TPU v7x, 32 devices: a whole 2x2x4 slice. The times are simulated.
32 devices in a mesh: pair: 8 (over z, y), band: 4 (over x, core).
Axes of the slice: x: 2, y: 2, z: 4, core: 2. Of those that a mesh axis runs over, the one named last changes fastest.
Arguments:
- orbitals: bfloat16 [2048, 23, 64], P('pair'), may hold values from -6 to 6
- screening: bfloat16 [1024, 8, 1024], P('pair', None, 'band'), may hold values from -0.1875 to 0.1875
- trial: bfloat16 [1024, 23, 64], P('pair'), may hold values from -6 to 6
- pair_kpts: int32 [8, 2], replicated, may hold values from 0 to 22
- pair_q: int32 [8], replicated, may hold values from 0 to 7
Outputs:
- applied: float32 [1024, 23, 64], P('pair', None, 'band')
All inputs are finite; a program needn't handle non-finite values.
Results may differ from a plain program's by a relative error of at most 0.013.
Values may be sent and summed in bfloat16 or wider, within the bound.
No kernel may reach another device: no remote copies, remote signals or barrier semaphores. Data moves between devices by JAX's collectives and lax.ppermute only.
A program may use at most 64 MiB of HBM per device.

v0:
```python
import math
import jax
import jax.numpy as jnp
from jax import lax
from jax.sharding import PartitionSpec as P

NV = 32
NC = 32
NR = 2048
NG = 1024
KPTS = 23
NB = 64


def basis_rows(first_row, row_count, point_count):
    frequency = first_row + jnp.arange(row_count, dtype=jnp.int32)
    position = jnp.arange(point_count, dtype=jnp.int32)
    phase_index = (2 * position[None, :] + 1) * frequency[:, None] % (4 * point_count)
    values = jnp.cos(phase_index.astype(jnp.float32) * (math.pi / (2 * point_count))) * math.sqrt(
        2.0 / point_count
    )
    return values.astype(jnp.bfloat16)


def densities(first_set, second_set):
    merged = first_set.astype(jnp.float32)[:, :, None] * second_set.astype(jnp.float32)[:, None, :]
    return merged.reshape(first_set.shape[0], first_set.shape[1] * second_set.shape[1]).astype(
        jnp.bfloat16
    )


def transform(basis_block, first_set, second_set):
    return lax.dot_general(
        basis_block,
        densities(first_set, second_set),
        (((1,), (0,)), ((), ())),
        preferred_element_type=jnp.float32,
    ).astype(jnp.bfloat16)


def on_device(orbitals, screening, trial, pair_kpts, pair_q):
    band_count = lax.axis_size("band")
    pair_count = lax.axis_size("pair")
    pair_here = lax.axis_index("pair")
    own_kpts = lax.dynamic_index_in_dim(pair_kpts, pair_here, 0, keepdims=False)
    listed = pair_kpts.shape[0]
    vector_count = trial.shape[2]
    orbital_send = orbitals[:, pair_kpts].reshape(orbitals.shape[0], listed, 2 * NB)
    trial_send = trial[:, pair_kpts].reshape(trial.shape[0], listed, 2 * vector_count)
    screen_send = screening[:, pair_q]
    orbital_got, trial_got, screen_got = (
        lax.all_to_all(orbital_send, "pair", split_axis=1, concat_axis=0, tiled=True),
        lax.all_to_all(trial_send, "pair", split_axis=1, concat_axis=0, tiled=True),
        lax.all_to_all(screen_send, "pair", split_axis=1, concat_axis=0, tiled=True),
    )
    screen_cols = screen_got[:, 0]
    first_orb = orbital_got[:, 0, :NB]
    second_orb = orbital_got[:, 0, NB:]
    row_count = NG // band_count
    basis_block = basis_rows(lax.axis_index("band") * row_count, row_count, NR)
    valence = transform(basis_block, first_orb[:, :NV], second_orb[:, :NV])
    conduction = transform(basis_block, first_orb[:, NV:], second_orb[:, NV:])
    screened = lax.dot_general(
        screen_cols,
        lax.all_gather(valence, "band", axis=0, tiled=True),
        (((0,), (0,)), ((), ())),
        preferred_element_type=jnp.float32,
    ).astype(jnp.bfloat16)
    raw = lax.dot_general(
        conduction, screened, (((0,), (0,)), ((), ())), preferred_element_type=jnp.float32
    ) * (1.0 / math.sqrt(NG))
    kernel = (
        raw.reshape(NC, NC, NV, NV)
        .transpose(2, 0, 3, 1)
        .reshape(NV * NC, NV * NC)
        .astype(jnp.bfloat16)
    )
    trial_first = trial_got[:, 0, :vector_count]
    trial_second = trial_got[:, 0, vector_count:]
    apply_scale = 1.0 / math.sqrt(NV * NC)
    forward = (
        lax.dot_general(
            kernel, trial_second, (((1,), (0,)), ((), ())), preferred_element_type=jnp.float32
        )
        * apply_scale
    )
    backward = (
        lax.dot_general(
            kernel, trial_first, (((0,), (0,)), ((), ())), preferred_element_type=jnp.float32
        )
        * apply_scale
    )
    partials = jnp.stack([forward, backward])
    summed = lax.psum_scatter(
        partials.astype(jnp.bfloat16), "band", scatter_dimension=2, tiled=True
    ).astype(jnp.float32)
    share = summed.shape[2]
    state_rows = summed.shape[1] // pair_count
    kpt_ids = jnp.arange(KPTS, dtype=jnp.int32)
    one_hot = (own_kpts[:, None] == kpt_ids[None, :]).astype(jnp.float32)
    spread = (
        summed[0][:, None, :] * one_hot[0][None, :, None]
        + summed[1][:, None, :] * one_hot[1][None, :, None]
    )
    spread = spread.reshape(summed.shape[1], KPTS * share)
    scattered = lax.psum_scatter(spread, "pair", scatter_dimension=0, tiled=True)
    return scattered.reshape(state_rows, KPTS, share)


def solution(mesh):
    return jax.shard_map(
        on_device,
        mesh=mesh,
        in_specs=(P("pair", None, None), P("pair", None, "band"), P("pair", None, None), P(), P()),
        out_specs=P("pair", None, "band"),
        check_vma=False,
    )
```

profile of v0, /device:TPU:0, one launch (start us, length us, event | category | flops | bytes accessed | tf_op | source)
XLA Modules:
  0.0 212.1 jit_solution(7176523066295668518)
XLA Ops:
  6.5 0.8 compare_select_fusion
  7.7 1.4 gather_fusion
  9.1 7.3 %all-to-all-start = ((bf16[256,8,128]{0,2,1:T(8,128)(2,1)}), bf16[256,8,128]{0,2,1:T(8,128)(2,1)S(1)}, u32[]{:S(2)}, u32[]{:S(2)}) async-start(bf16[256,8,128]{0,2,1:T(8,128)(2,1)} %bitcast.2), calls=%async_computation | async-start | bytes 1048576 | tf_op jit(solution)/shard_map/all_to_all | solution.py:52
  16.4 14.4 %all-to-all-done = bf16[256,8,128]{0,2,1:T(8,128)(2,1)S(1)} async-done(((bf16[256,8,128]{0,2,1:T(8,128)(2,1)}), bf16[256,8,128]{0,2,1:T(8,128)(2,1)S(1)}, u32[]{:S(2)}, u32[]{:S(2)}) %all-to-all-start) | async-done | bytes 524320 | tf_op jit(solution)/shard_map/all_to_all | solution.py:52
  31.8 4.2 %multiply_convert_fusion = (bf16[2048,32,32]{0,2,1:T(8,128)(2,1)S(1)}, bf16[2048,32,32]{0,2,1:T(8,128)(2,1)}) fusion(f32[2048,32]{0,1:T(8,128)S(1)} %get-tuple-element.9, f32[2048,32]{0,1:T(8,128)S(1)} %get-tuple-element.7, f32[2048,32]{0,1:T(8,128)S(1)} %get-tuple-element.10, f32[2048,32]{0,1:T(8,128)S(1)} %get-tuple-element.8), kind=kLoop, calls=%fused_computation.3 | loop fusion | flops 8388608 | bytes 9437184 | tf_op jit(solution)/shard_map/convert_element_type | solution.py:27
  36.0 10.2 %convolution_convert_fusion.1 = bf16[256,1024]{1,0:T(8,128)(2,1)} fusion(bf16[2048,1024]{0,1:T(8,128)(2,1)S(1)} %bitcast.70, s32[256]{0:T(256)S(1)} %iota_add_fusion, s32[2048]{0:T(1024)S(1)} %multiply_add_fusion), kind=kOutput, calls=%fused_computation.21 | convolution fusion | flops 1082392576 | bytes 4727808 | tf_op jit(solution)/shard_map/dot_general | solution.py:33
  46.3 1.3 gather_fusion.2
  47.6 3.6 %all-to-all-start.2 = ((bf16[128,8,128]{0,2,1:T(8,128)(2,1)}), bf16[128,8,128]{0,2,1:T(8,128)(2,1)S(1)}, u32[]{:S(2)}, u32[]{:S(2)}) async-start(bf16[128,8,128]{0,2,1:T(8,128)(2,1)} %bitcast.17), calls=%async_computation.2 | async-start | bytes 524288 | tf_op jit(solution)/shard_map/all_to_all | solution.py:53
  51.3 2.0 gather_fusion.1
  53.3 0.9 copy.29
  54.2 6.1 %all-to-all-done.2 = bf16[128,8,128]{0,2,1:T(8,128)(2,1)S(1)} async-done(((bf16[128,8,128]{0,2,1:T(8,128)(2,1)}), bf16[128,8,128]{0,2,1:T(8,128)(2,1)S(1)}, u32[]{:S(2)}, u32[]{:S(2)}) %all-to-all-start.2) | async-done | bytes 262176 | tf_op jit(solution)/shard_map/all_to_all | solution.py:53
  60.3 3.6 %all-to-all-start.1 = ((bf16[128,8,256]{2,0,1:T(8,128)(2,1)}), bf16[128,8,256]{2,0,1:T(8,128)(2,1)S(1)}, u32[]{:S(2)}, u32[]{:S(2)}) async-start(bf16[128,8,256]{2,0,1:T(8,128)(2,1)} %copy.29), calls=%async_computation.1 | async-start | bytes 1048576 | tf_op jit(solution)/shard_map/all_to_all | solution.py:54
  64.3 11.5 %convolution_convert_fusion.2 = bf16[256,1024]{1,0:T(8,128)(2,1)} fusion(bf16[2048,1024]{0,1:T(8,128)(2,1)} %bitcast.69, s32[256]{0:T(256)S(1)} %iota_add_fusion, s32[2048]{0:T(1024)S(1)} %multiply_add_fusion), kind=kOutput, calls=%fused_computation.22 | convolution fusion | flops 1082392576 | bytes 4727808 | tf_op jit(solution)/shard_map/dot_general | solution.py:33
  75.8 2.3 %all-to-all-done.1 = bf16[128,8,256]{2,0,1:T(8,128)(2,1)S(1)} async-done(((bf16[128,8,256]{2,0,1:T(8,128)(2,1)}), bf16[128,8,256]{2,0,1:T(8,128)(2,1)S(1)}, u32[]{:S(2)}, u32[]{:S(2)}) %all-to-all-start.1) | async-done | bytes 524320 | tf_op jit(solution)/shard_map/all_to_all | solution.py:54
  78.1 0.8 copy-done.3
  78.9 3.3 %multiply_convert_fusion.2 = bf16[1024,1024]{1,0:T(8,128)(2,1)S(1)} fusion(bf16[256,1024]{1,0:T(8,128)(2,1)} %convolution_convert_fusion.2, bf16[1024,256]{1,0:T(8,128)(2,1)} %bitcast.78, bf16[1024,1024]{1,0:T(8,128)(2,1)} %all-gather.2.cloned.1.call-done), kind=kOutput, calls=%fused_computation.5 | convolution fusion | flops 1076101120 | bytes 5242880 | tf_op jit(solution)/shard_map/dot_general | solution.py:69
  82.2 8.2 %convert_element_type.73 = bf16[32,32,32,32]{3,2,1,0:T(8,128)(2,1)} reshape(bf16[1024,1024]{1,0:T(8,128)(2,1)S(1)} %multiply_convert_fusion.2) | data formatting | bytes 4194304 | tf_op jit(solution)/shard_map/convert_element_type | solution.py:76
  90.4 15.2 %copy.30 = bf16[32,32,32,32]{1,3,0,2:T(8,128)(2,1)} copy(bf16[32,32,32,32]{3,2,1,0:T(8,128)(2,1)} %convert_element_type.73) | data formatting | bytes 4194304 | tf_op jit(solution)/shard_map/convert_element_type | solution.py:76
  105.6 11.3 %convert_element_type.75 = bf16[1024,1024]{1,0:T(8,128)(2,1)S(1)} reshape(bf16[32,32,32,32]{3,2,1,0:T(8,128)(2,1)} %bitcast.67) | data formatting | bytes 4194304 | tf_op jit(solution)/shard_map/convert_element_type | solution.py:76
  116.9 0.8 fusion.10
  119.7 18.6 %reduce-scatter.3.cloned.1.call-done = bf16[2,1024,16]{1,2,0:T(8,128)(2,1)} async-done(((bf16[2,1024,64]{1,2,0:T(8,128)(2,1)}), bf16[2,1024,16]{1,2,0:T(8,128)(2,1)}) %reduce-scatter.3.cloned.1.call-update) | async-done | bytes 65552 | tf_op jit(solution)/shard_map/reduce_scatter | solution.py:94
  138.3 0.8 convert_element_type.76
  139.2 1.4 fusion.6
  140.6 65.0 %reduce-scatter.5.cloned.1.call-done = f32[128,368]{0,1:T(8,128)} async-done(((f32[1024,368]{0,1:T(8,128)}), f32[128,368]{0,1:T(8,128)}) %reduce-scatter.5.cloned.1.call-update) | async-done | bytes 188432 | tf_op jit(solution)/shard_map/reduce_scatter | solution.py:106
  (42 shorter events, 3.7 us)
Async XLA Ops:
  6.5 1.1 copy-start
  9.1 21.8 %all-to-all-start = ((bf16[256,8,128]{0,2,1:T(8,128)(2,1)}), bf16[256,8,128]{0,2,1:T(8,128)(2,1)S(1)}, u32[]{:S(2)}, u32[]{:S(2)}) async-start(bf16[256,8,128]{0,2,1:T(8,128)(2,1)} %bitcast.2), calls=%async_computation | async-start | bytes 1048576 | tf_op jit(solution)/shard_map/all_to_all | solution.py:52
  16.4 61.8 %all-gather.2.cloned.1.call-start = ((), (), s32[]{:S(2)}) async-start(), calls=%async_computation.5 | async-start | bytes 2621440 | tf_op jit(solution)/shard_map/all_gather | solution.py:65
  36.0 10.2 %copy-start.2 = (bf16[128,23,64]{0,2,1:T(8,128)(2,1)S(1)}, bf16[128,23,64]{0,2,1:T(8,128)(2,1)}, u32[]{:S(2)}) copy-start(bf16[128,23,64]{0,2,1:T(8,128)(2,1)} %param.7) | copy-start | bytes 1130500
  46.2 5.0 %copy-start.5 = (s32[8]{0:T(128)S(1)}, s32[8]{0:T(128)}, u32[]{:S(2)}) copy-start(s32[8]{0:T(128)} %param.9) | copy-start | bytes 100
  46.2 5.0 %copy-start.1 = (bf16[128,8,256]{2,1,0:T(8,128)(2,1)S(1)}, bf16[128,8,256]{2,1,0:T(8,128)(2,1)}, u32[]{:S(2)}) copy-start(bf16[128,8,256]{2,1,0:T(8,128)(2,1)} %param.6) | copy-start | bytes 1572868
  47.6 12.7 %all-to-all-start.2 = ((bf16[128,8,128]{0,2,1:T(8,128)(2,1)}), bf16[128,8,128]{0,2,1:T(8,128)(2,1)S(1)}, u32[]{:S(2)}, u32[]{:S(2)}) async-start(bf16[128,8,128]{0,2,1:T(8,128)(2,1)} %bitcast.17), calls=%async_computation.2 | async-start | bytes 524288 | tf_op jit(solution)/shard_map/all_to_all | solution.py:53
  60.3 17.8 %all-to-all-start.1 = ((bf16[128,8,256]{2,0,1:T(8,128)(2,1)}), bf16[128,8,256]{2,0,1:T(8,128)(2,1)S(1)}, u32[]{:S(2)}, u32[]{:S(2)}) async-start(bf16[128,8,256]{2,0,1:T(8,128)(2,1)} %copy.29), calls=%async_computation.1 | async-start | bytes 1048576 | tf_op jit(solution)/shard_map/all_to_all | solution.py:54
  63.9 74.4 %reduce-scatter.3.cloned.1.call-start = ((), (), s32[]{:S(2)}) async-start(), calls=%async_computation.6 | async-start | bytes 327680 | tf_op jit(solution)/shard_map/reduce_scatter | solution.py:94
  78.1 0.8 copy-start.3
  117.7 1.3 copy-start.4
  119.0 86.5 %reduce-scatter.5.cloned.1.call-start = ((), (), s32[]{:S(2)}) async-start(), calls=%async_computation.7 | async-start | bytes 1695744 | tf_op jit(solution)/shard_map/reduce_scatter | solution.py:106
Sparse Core Ops, SparseCore 0:
  46.4 21.6 all-gather.1
  119.1 19.1 reduce-scatter.2
  141.7 63.7 reduce-scatter.4
where the time goes:
time: 213 us; the launch traced here: 212 us
  waiting for transfers between devices  106 us (50%)
  local copies, waits for them, and re-layouts  43.1 us (20%)
  matrix products  26.3 us (12%)
  starting transfers between devices  14.8 us (7%)
  between operations  13.3 us (6%)
  other arithmetic  8.09 us (4%)
    reduce_scatter x1, waiting for transfers between devices, on_device(): lax.psum_scatter(spread, 'pair', scatter_dimension=0, tiled=True)  65 us
    convert_element_type x3, local copies, waits for them, and re-layouts, on_device(): kernel = raw.reshape(NC, NC, NV, NV).transpose(2, 0, 3, 1).reshape(NV * N...  34.7 us
    dot_general x2, matrix products, transform(): lax.dot_general(basis_block, densities(first_set, second_set), (((1,), (0...  21.7 us
    reduce_scatter x1, waiting for transfers between devices, on_device(): lax.psum_scatter(partials.astype(jnp.bfloat16), 'band', scatter_dimension...  18.6 us
    all_to_all x1, waiting for transfers between devices, on_device(): lax.all_to_all(orbital_send, 'pair', split_axis=1, concat_axis=0, tiled=T...  14.4 us
    all_to_all x1, starting transfers between devices, on_device(): lax.all_to_all(orbital_send, 'pair', split_axis=1, concat_axis=0, tiled=T...  7.31 us
    all_to_all x1, waiting for transfers between devices, on_device(): lax.all_to_all(trial_send, 'pair', split_axis=1, concat_axis=0, tiled=True)  6.1 us
  transfers between devices with their start and end apart: 6, of which 5 were waited for; matrix products, arithmetic and copies ran while one was open for 8% of the time, Pallas kernels for 0%

commit v1 on v0

--- a/solution.py
+++ b/solution.py
@@ -10,6 +10,18 @@
 NG = 1024
 KPTS = 23
 NB = 64
+
+
+def sent_to_each(x, axis, split, join):
+    ways, here = (lax.axis_size(axis), lax.axis_index(axis))
+    width = x.shape[split] // ways
+    turned = jnp.roll(x, -here * width, axis=split)
+    got = [lax.slice_in_dim(turned, 0, width, axis=split)]
+    for far in range(1, ways):
+        sent = lax.slice_in_dim(turned, far * width, (far + 1) * width, axis=split)
+        got.append(lax.ppermute(sent, axis, [(d, (d + far) % ways) for d in range(ways)]))
+    line = jnp.concatenate(got[::-1], axis=join)
+    return jnp.roll(line, (here + 1) * got[0].shape[join], axis=join)
 
 
 def basis_rows(first_row, row_count, point_count):
@@ -49,7 +61,7 @@
     trial_send = trial[:, pair_kpts].reshape(trial.shape[0], listed, 2 * vector_count)
     screen_send = screening[:, pair_q]
     orbital_got, trial_got, screen_got = (
-        lax.all_to_all(orbital_send, "pair", split_axis=1, concat_axis=0, tiled=True),
+        sent_to_each(orbital_send, "pair", 1, 0),
         lax.all_to_all(trial_send, "pair", split_axis=1, concat_axis=0, tiled=True),
         lax.all_to_all(screen_send, "pair", split_axis=1, concat_axis=0, tiled=True),
     )

time: 213 us -> 206 us (0.967)
  waiting for transfers between devices: 106 us -> 98.5 us
  starting transfers between devices: 14.8 us -> 19.8 us
    all_to_all x1 -> x0, waiting for transfers between devices: 14.4 us -> none  [on_device(): lax.all_to_all(orbital_send, 'pair', split_axis=1, concat_axis=0, tiled=T...]
    ppermute x0 -> x7, starting transfers between devices: none -> 12.6 us  [sent_to_each(): lax.ppermute(sent, axis, [(d, (d + far) % ways) for d in range(ways)])]
    ppermute x0 -> x7, waiting for transfers between devices: none -> 7.49 us  [sent_to_each(): lax.ppermute(sent, axis, [(d, (d + far) % ways) for d in range(ways)])]
    all_to_all x1 -> x0, starting transfers between devices: 7.31 us -> none  [on_device(): lax.all_to_all(orbital_send, 'pair', split_axis=1, concat_axis=0, tiled=T...]
  transfers between devices with their start and end apart: 6 -> 12, of which waited for: 5 -> 6; matrix products, arithmetic and copies ran while one was open for 8% -> 8% of each run, Pallas kernels for 0% -> 0%
where the time goes in v1:
time: 206 us; the launch traced here: 205 us
  waiting for transfers between devices  98.5 us (48%)
  local copies, waits for them, and re-layouts  41.1 us (20%)
  matrix products  25.1 us (12%)
  starting transfers between devices  19.8 us (10%)
  between operations  13.4 us (7%)
  other arithmetic  6.91 us (3%)
    reduce_scatter x1, waiting for transfers between devices, on_device(): lax.psum_scatter(spread, 'pair', scatter_dimension=0, tiled=True)  65 us
    convert_element_type x3, local copies, waits for them, and re-layouts, on_device(): kernel = raw.reshape(NC, NC, NV, NV).transpose(2, 0, 3, 1).reshape(NV * N...  34.5 us
    dot_general x2, matrix products, transform(): lax.dot_general(basis_block, densities(first_set, second_set), (((1,), (0...  20.4 us
    reduce_scatter x1, waiting for transfers between devices, on_device(): lax.psum_scatter(partials.astype(jnp.bfloat16), 'band', scatter_dimension...  18.7 us
    ppermute x7, starting transfers between devices, sent_to_each(): lax.ppermute(sent, axis, [(d, (d + far) % ways) for d in range(ways)])  12.6 us
    ppermute x7, waiting for transfers between devices, sent_to_each(): lax.ppermute(sent, axis, [(d, (d + far) % ways) for d in range(ways)])  7.49 us
    all_to_all x1, waiting for transfers between devices, on_device(): lax.all_to_all(trial_send, 'pair', split_axis=1, concat_axis=0, tiled=True)  5.21 us
  transfers between devices with their start and end apart: 12, of which 6 were waited for; matrix products, arithmetic and copies ran while one was open for 8% of the time, Pallas kernels for 0%

profile of v1, /device:TPU:0, one launch (start us, length us, event | category | flops | bytes accessed | tf_op | source)
XLA Modules:
  0.0 204.8 jit_solution(17450906032185378614)
XLA Ops:
  9.0 6.1 %collective-permute-start = (bf16[256,1,128]{0,2,1:T(8,128)(2,1)S(1)}, bf16[256,1,128]{0,2,1:T(8,128)(2,1)S(1)}, u32[]{:S(2)}, u32[]{:S(2)}) collective-permute-start(bf16[256,1,128]{0,2,1:T(8,128)(2,1)S(1)} %get-tuple-element.13), channel_id=1, source_target_pairs={{0,28},{4,0},{8,4},{12,8},{16,12},{20,16},{24,20},{28,24},{1,29},{... | collective-permute-start | bytes 196616 | tf_op jit(solution)/shard_map/ppermute | solution.py:22
  15.5 3.0 %collective-permute-start.3 = (bf16[256,1,128]{0,2,1:T(8,128)(2,1)S(1)}, bf16[256,1,128]{0,2,1:T(8,128)(2,1)S(1)}, u32[]{:S(2)}, u32[]{:S(2)}) collective-permute-start(bf16[256,1,128]{0,2,1:T(8,128)(2,1)S(1)} %get-tuple-element.10), channel_id=1, source_target_pairs={{0,16},{4,20},{8,24},{12,28},{16,0},{20,4},{24,8},{28,12},{1,17},{... | collective-permute-start | bytes 196616 | tf_op jit(solution)/shard_map/ppermute | solution.py:22
  18.5 1.9 collective-permute-start.5
  20.4 1.2 collective-permute-start.6
  21.6 4.8 %collective-permute-done.3 = bf16[256,1,128]{0,2,1:T(8,128)(2,1)S(1)} collective-permute-done((bf16[256,1,128]{0,2,1:T(8,128)(2,1)S(1)}, bf16[256,1,128]{0,2,1:T(8,128)(2,1)S(1)}, u32[]{:S(2)}, u32[]{:S(2)}) %collective-permute-start.3) | collective-permute-done | bytes 65568 | tf_op jit(solution)/shard_map/ppermute | solution.py:22
  26.4 2.7 %collective-permute-done.4 = bf16[256,1,128]{0,2,1:T(8,128)(2,1)S(1)} collective-permute-done((bf16[256,1,128]{0,2,1:T(8,128)(2,1)S(1)}, bf16[256,1,128]{0,2,1:T(8,128)(2,1)S(1)}, u32[]{:S(2)}, u32[]{:S(2)}) %collective-permute-start.4) | collective-permute-done | bytes 65568 | tf_op jit(solution)/shard_map/ppermute | solution.py:22
  29.5 1.1 multiply_convert_fusion
  30.6 10.2 %convolution_convert_fusion.1 = bf16[256,1024]{1,0:T(8,128)(2,1)} fusion(bf16[2048,1024]{0,1:T(8,128)(2,1)S(1)} %bitcast.68, s32[256]{0:T(256)S(1)} %iota_add_fusion, s32[2048]{0:T(1024)S(1)} %multiply_add_fusion), kind=kOutput, calls=%fused_computation.21 | convolution fusion | flops 1082392576 | bytes 4727808 | tf_op jit(solution)/shard_map/dot_general | solution.py:45
  40.8 1.3 gather_fusion.2
  42.1 3.4 %all-to-all-start.1 = ((bf16[128,8,128]{0,2,1:T(8,128)(2,1)}), bf16[128,8,128]{0,2,1:T(8,128)(2,1)S(1)}, u32[]{:S(2)}, u32[]{:S(2)}) async-start(bf16[128,8,128]{0,2,1:T(8,128)(2,1)} %bitcast.14), calls=%async_computation.1 | async-start | bytes 524288 | tf_op jit(solution)/shard_map/all_to_all | solution.py:65
  45.5 2.0 gather_fusion.1
  47.6 0.9 copy.24
  48.5 5.2 %all-to-all-done.1 = bf16[128,8,128]{0,2,1:T(8,128)(2,1)S(1)} async-done(((bf16[128,8,128]{0,2,1:T(8,128)(2,1)}), bf16[128,8,128]{0,2,1:T(8,128)(2,1)S(1)}, u32[]{:S(2)}, u32[]{:S(2)}) %all-to-all-start.1) | async-done | bytes 262176 | tf_op jit(solution)/shard_map/all_to_all | solution.py:65
  53.7 3.5 %all-to-all-start = ((bf16[128,8,256]{2,0,1:T(8,128)(2,1)}), bf16[128,8,256]{2,0,1:T(8,128)(2,1)S(1)}, u32[]{:S(2)}, u32[]{:S(2)}) async-start(bf16[128,8,256]{2,0,1:T(8,128)(2,1)} %copy.24), calls=%async_computation | async-start | bytes 1048576 | tf_op jit(solution)/shard_map/all_to_all | solution.py:66
  57.4 1.1 multiply_convert_fusion.1
  58.5 10.2 %convolution_convert_fusion.2 = bf16[256,1024]{1,0:T(8,128)(2,1)} fusion(bf16[2048,1024]{0,1:T(8,128)(2,1)S(1)} %bitcast.67, s32[256]{0:T(256)S(1)} %iota_add_fusion, s32[2048]{0:T(1024)S(1)} %multiply_add_fusion), kind=kOutput, calls=%fused_computation.22 | convolution fusion | flops 1082392576 | bytes 4727808 | tf_op jit(solution)/shard_map/dot_general | solution.py:45
  68.9 2.0 all-to-all-done
  71.7 3.3 %multiply_convert_fusion.2 = bf16[1024,1024]{1,0:T(8,128)(2,1)S(1)} fusion(bf16[256,1024]{1,0:T(8,128)(2,1)} %convolution_convert_fusion.2, bf16[1024,256]{1,0:T(8,128)(2,1)} %bitcast.73, bf16[1024,1024]{1,0:T(8,128)(2,1)} %all-gather.2.cloned.1.call-done), kind=kOutput, calls=%fused_computation.5 | convolution fusion | flops 1076101120 | bytes 5242880 | tf_op jit(solution)/shard_map/dot_general | solution.py:81
  75.0 7.9 %convert_element_type.73 = bf16[32,32,32,32]{3,2,1,0:T(8,128)(2,1)} reshape(bf16[1024,1024]{1,0:T(8,128)(2,1)S(1)} %multiply_convert_fusion.2) | data formatting | bytes 4194304 | tf_op jit(solution)/shard_map/convert_element_type | solution.py:88
  82.9 15.2 %copy.25 = bf16[32,32,32,32]{1,3,0,2:T(8,128)(2,1)} copy(bf16[32,32,32,32]{3,2,1,0:T(8,128)(2,1)} %convert_element_type.73) | data formatting | bytes 4194304 | tf_op jit(solution)/shard_map/convert_element_type | solution.py:88
  98.1 11.3 %convert_element_type.75 = bf16[1024,1024]{1,0:T(8,128)(2,1)S(1)} reshape(bf16[32,32,32,32]{3,2,1,0:T(8,128)(2,1)} %bitcast.65) | data formatting | bytes 4194304 | tf_op jit(solution)/shard_map/convert_element_type | solution.py:88
  112.2 18.7 %reduce-scatter.3.cloned.1.call-done = bf16[2,1024,16]{1,2,0:T(8,128)(2,1)} async-done(((bf16[2,1024,64]{1,2,0:T(8,128)(2,1)}), bf16[2,1024,16]{1,2,0:T(8,128)(2,1)}) %reduce-scatter.3.cloned.1.call-update) | async-done | bytes 65552 | tf_op jit(solution)/shard_map/reduce_scatter | solution.py:106
  131.8 1.4 fusion.6
  133.2 65.0 %reduce-scatter.5.cloned.1.call-done = f32[128,368]{0,1:T(8,128)} async-done(((f32[1024,368]{0,1:T(8,128)}), f32[128,368]{0,1:T(8,128)}) %reduce-scatter.5.cloned.1.call-update) | async-done | bytes 188432 | tf_op jit(solution)/shard_map/reduce_scatter | solution.py:118
  (67 shorter events, 7.9 us)
Async XLA Ops:
  6.5 1.6 copy-start
  6.5 64.4 %all-gather.2.cloned.1.call-start = ((), (), s32[]{:S(2)}) async-start(), calls=%async_computation.4 | async-start | bytes 2621440 | tf_op jit(solution)/shard_map/all_gather | solution.py:77
  9.0 9.5 %collective-permute-start = (bf16[256,1,128]{0,2,1:T(8,128)(2,1)S(1)}, bf16[256,1,128]{0,2,1:T(8,128)(2,1)S(1)}, u32[]{:S(2)}, u32[]{:S(2)}) collective-permute-start(bf16[256,1,128]{0,2,1:T(8,128)(2,1)S(1)} %get-tuple-element.13), channel_id=1, source_target_pairs={{0,28},{4,0},{8,4},{12,8},{16,12},{20,16},{24,20},{28,24},{1,29},{... | collective-permute-start | bytes 196616 | tf_op jit(solution)/shard_map/ppermute | solution.py:22
  15.1 5.4 %collective-permute-start.1 = (bf16[256,1,128]{0,2,1:T(8,128)(2,1)S(1)}, bf16[256,1,128]{0,2,1:T(8,128)(2,1)S(1)}, u32[]{:S(2)}, u32[]{:S(2)}) collective-permute-start(bf16[256,1,128]{0,2,1:T(8,128)(2,1)S(1)} %get-tuple-element.12), channel_id=1, source_target_pairs={{0,24},{4,28},{8,0},{12,4},{16,8},{20,12},{24,16},{28,20},{1,25},{... | collective-permute-start | bytes 196616 | tf_op jit(solution)/shard_map/ppermute | solution.py:22
  15.5 6.1 %collective-permute-start.2 = (bf16[256,1,128]{0,2,1:T(8,128)(2,1)S(1)}, bf16[256,1,128]{0,2,1:T(8,128)(2,1)S(1)}, u32[]{:S(2)}, u32[]{:S(2)}) collective-permute-start(bf16[256,1,128]{0,2,1:T(8,128)(2,1)S(1)} %get-tuple-element.11), channel_id=1, source_target_pairs={{0,20},{4,24},{8,28},{12,0},{16,4},{20,8},{24,12},{28,16},{1,21},{... | collective-permute-start | bytes 196616 | tf_op jit(solution)/shard_map/ppermute | solution.py:22
  15.5 10.9 %collective-permute-start.3 = (bf16[256,1,128]{0,2,1:T(8,128)(2,1)S(1)}, bf16[256,1,128]{0,2,1:T(8,128)(2,1)S(1)}, u32[]{:S(2)}, u32[]{:S(2)}) collective-permute-start(bf16[256,1,128]{0,2,1:T(8,128)(2,1)S(1)} %get-tuple-element.10), channel_id=1, source_target_pairs={{0,16},{4,20},{8,24},{12,28},{16,0},{20,4},{24,8},{28,12},{1,17},{... | collective-permute-start | bytes 196616 | tf_op jit(solution)/shard_map/ppermute | solution.py:22
  18.5 10.6 %collective-permute-start.4 = (bf16[256,1,128]{0,2,1:T(8,128)(2,1)S(1)}, bf16[256,1,128]{0,2,1:T(8,128)(2,1)S(1)}, u32[]{:S(2)}, u32[]{:S(2)}) collective-permute-start(bf16[256,1,128]{0,2,1:T(8,128)(2,1)S(1)} %get-tuple-element.9), channel_id=1, source_target_pairs={{0,12},{4,16},{8,20},{12,24},{16,28},{20,0},{24,4},{28,8},{1,13},{... | collective-permute-start | bytes 196616 | tf_op jit(solution)/shard_map/ppermute | solution.py:22
  18.5 10.6 %collective-permute-start.5 = (bf16[256,1,128]{0,2,1:T(8,128)(2,1)S(1)}, bf16[256,1,128]{0,2,1:T(8,128)(2,1)S(1)}, u32[]{:S(2)}, u32[]{:S(2)}) collective-permute-start(bf16[256,1,128]{0,2,1:T(8,128)(2,1)S(1)} %get-tuple-element.8), channel_id=1, source_target_pairs={{0,8},{4,12},{8,16},{12,20},{16,24},{20,28},{24,0},{28,4},{1,9},{5... | collective-permute-start | bytes 196616 | tf_op jit(solution)/shard_map/ppermute | solution.py:22
  20.4 8.7 %collective-permute-start.6 = (bf16[256,1,128]{0,2,1:T(8,128)(2,1)S(1)}, bf16[256,1,128]{0,2,1:T(8,128)(2,1)S(1)}, u32[]{:S(2)}, u32[]{:S(2)}) collective-permute-start(bf16[256,1,128]{0,2,1:T(8,128)(2,1)S(1)} %get-tuple-element.7), channel_id=1, source_target_pairs={{0,4},{4,8},{8,12},{12,16},{16,20},{20,24},{24,28},{28,0},{1,5},{5... | collective-permute-start | bytes 196616 | tf_op jit(solution)/shard_map/ppermute | solution.py:22
  30.5 10.3 %copy-start.2 = (bf16[128,23,64]{0,2,1:T(8,128)(2,1)S(1)}, bf16[128,23,64]{0,2,1:T(8,128)(2,1)}, u32[]{:S(2)}) copy-start(bf16[128,23,64]{0,2,1:T(8,128)(2,1)} %param.7) | copy-start | bytes 1130500
  40.8 4.8 %copy-start.1 = (bf16[128,8,256]{2,1,0:T(8,128)(2,1)S(1)}, bf16[128,8,256]{2,1,0:T(8,128)(2,1)}, u32[]{:S(2)}) copy-start(bf16[128,8,256]{2,1,0:T(8,128)(2,1)} %param.6) | copy-start | bytes 1572868
  42.1 11.6 %all-to-all-start.1 = ((bf16[128,8,128]{0,2,1:T(8,128)(2,1)}), bf16[128,8,128]{0,2,1:T(8,128)(2,1)S(1)}, u32[]{:S(2)}, u32[]{:S(2)}) async-start(bf16[128,8,128]{0,2,1:T(8,128)(2,1)} %bitcast.14), calls=%async_computation.1 | async-start | bytes 524288 | tf_op jit(solution)/shard_map/all_to_all | solution.py:65
  53.7 17.2 %all-to-all-start = ((bf16[128,8,256]{2,0,1:T(8,128)(2,1)}), bf16[128,8,256]{2,0,1:T(8,128)(2,1)S(1)}, u32[]{:S(2)}, u32[]{:S(2)}) async-start(bf16[128,8,256]{2,0,1:T(8,128)(2,1)} %copy.24), calls=%async_computation | async-start | bytes 1048576 | tf_op jit(solution)/shard_map/all_to_all | solution.py:66
  57.2 73.7 %reduce-scatter.3.cloned.1.call-start = ((), (), s32[]{:S(2)}) async-start(), calls=%async_computation.5 | async-start | bytes 327680 | tf_op jit(solution)/shard_map/reduce_scatter | solution.py:106
  70.9 0.8 copy-start.3
  110.3 1.3 copy-start.4
  111.5 86.7 %reduce-scatter.5.cloned.1.call-start = ((), (), s32[]{:S(2)}) async-start(), calls=%async_computation.6 | async-start | bytes 1695744 | tf_op jit(solution)/shard_map/reduce_scatter | solution.py:118
Sparse Core Ops, SparseCore 0:
  40.9 20.2 all-gather.1
  111.7 19.2 reduce-scatter.2
  134.4 63.7 reduce-scatter.4
